TPU v7x, 512 devices: a whole 4x8x8 slice. The times are simulated.
512 devices in a mesh: db: 64 (over y, z), heads: 8 (over x, core).
Axes of the slice: x: 4, y: 8, z: 8, core: 2. Of those that a mesh axis runs over, the one named last changes fastest.
Arguments:
- queries: bfloat16 [32768, 3072], P('db', 'heads'), may hold values from -80 to 80
- neighbour_ids: int32 [512, 2], P('db'), may hold values from 0 to 383, as said below
- cache_keys: bfloat16 [384, 128, 1024], P('db', None, 'heads'), may hold values from -16 to 16
- cache_values: bfloat16 [384, 128, 1024], P('db', None, 'heads'), may hold values from -6 to 6
- out_grad: bfloat16 [32768, 3072], P('db', 'heads'), may hold values from -6 to 6
Outputs:
- query_grad: bfloat16 [32768, 3072], P('db', 'heads')
Inputs may be any that keep to these rules, and one draw needn't show every extreme that they name: `neighbour_ids`: entry e is held by index floor(e / 6) of db. Among the 16 neighbours of the spans of one index of db (aligned blocks of 8 rows), at most 2 are held by any one index of db, and one index of db, the same for every block, holds exactly 2 of them in every block. Every other index of db holds at most one neighbour of a block.
All inputs are finite; a program needn't handle non-finite values.
Results may differ from a plain program's by a relative error of at most 0.014.
Values may be sent and summed in bfloat16 or wider, within the bound.
No kernel may reach another device: no remote copies, remote signals or barrier semaphores. Data moves between devices by JAX's collectives and lax.ppermute only.
A program may use at most 64 MiB of HBM per device.

v0:
```python
import math

import jax
import jax.numpy as jnp
from jax import lax
from jax.sharding import PartitionSpec as P

HD = 128
GROUP = 3
SPAN = 64
LENGTH = 4096


def shifted_2(block, axis, distance):
    devices = range(lax.axis_size(axis))
    route = [(i - distance, i) for i in devices if i - distance in devices]
    return lax.ppermute(block, axis, route)


def ranks(holder_list):
    number = holder_list.shape[0]
    position = jnp.arange(number, dtype=jnp.int32)
    earlier = (holder_list[:, None] == holder_list[None, :]) & (
        position[None, :] < position[:, None]
    )
    return jnp.sum(earlier.astype(jnp.int32), axis=1)


def attend(query_block, grad_block, key_rows, value_rows, valid_rows):
    factor = 1.0 / math.sqrt(query_block.shape[-1])
    scores = (
        jnp.einsum("bihgd,bkhd->bhgik", query_block, key_rows, preferred_element_type=jnp.float32)
        * factor
    )
    highest = jnp.max(scores, axis=-1, keepdims=True)
    expo = jnp.exp(scores - highest)
    probs = expo / jnp.sum(expo, axis=-1, keepdims=True)
    probs = jnp.where(valid_rows[:, None, None, :, None], probs, 0.0)
    probs_low = probs.astype(jnp.bfloat16)
    attended = jnp.einsum(
        "bhgik,bkhd->bihgd", probs_low, value_rows, preferred_element_type=jnp.float32
    ).astype(jnp.bfloat16)
    along = jnp.einsum(
        "bihgd,bkhd->bhgik", grad_block, value_rows, preferred_element_type=jnp.float32
    )
    delta = jnp.einsum(
        "bihgd,bihgd->bhgi", grad_block, attended, preferred_element_type=jnp.float32
    )
    slope = (probs * (along - delta[..., None])).astype(jnp.bfloat16)
    result = (
        jnp.einsum("bhgik,bkhd->bihgd", slope, key_rows, preferred_element_type=jnp.float32)
        * factor
    )
    return result.astype(jnp.bfloat16)


def attend_blocks(query_block, grad_block, key_rows, value_rows, valid_rows):
    number = query_block.shape[0]
    group_size = 8

    def one_group(operands):
        return attend(*operands)

    grouped = tuple(
        (
            item.reshape((number // group_size, group_size) + item.shape[1:])
            for item in (query_block, grad_block, key_rows, value_rows, valid_rows)
        )
    )
    result = lax.map(one_group, grouped)
    return result.reshape((number,) + result.shape[2:])


def fetch_slots(asked, cache_keys, cache_values, slot_index, holders_all, capacity):
    entry_rows = cache_keys.shape[1]
    channels = cache_keys.shape[2]
    picked = jnp.maximum(asked, 0).reshape(holders_all * capacity)
    send_keys = jnp.take(cache_keys, picked, axis=0).reshape(
        holders_all, capacity, entry_rows, channels
    )
    send_values = jnp.take(cache_values, picked, axis=0).reshape(
        holders_all, capacity, entry_rows, channels
    )
    got_keys, got_values = (
        lax.all_to_all(send_keys, "db", split_axis=0, concat_axis=0, tiled=True),
        lax.all_to_all(send_values, "db", split_axis=0, concat_axis=0, tiled=True),
    )
    own_keys = jnp.take(
        got_keys.reshape(holders_all * capacity, entry_rows, channels), slot_index, axis=0
    )
    own_values = jnp.take(
        got_values.reshape(holders_all * capacity, entry_rows, channels), slot_index, axis=0
    )
    return (own_keys, own_values)


def body(queries, neighbour_ids, cache_keys, cache_values, out_grad):
    holders_all = lax.axis_size("db")
    my_index = lax.axis_index("db")
    held_count = cache_keys.shape[0]
    entry_rows = cache_keys.shape[1]
    channels = cache_keys.shape[2]
    tokens_here = queries.shape[0]
    row_width = queries.shape[1]
    spans_here = neighbour_ids.shape[0]
    wanted_count = 2 * spans_here
    capacity = max(2, (wanted_count + holders_all - 1) // holders_all)
    kv_heads = channels // HD
    half_shift = tokens_here // 2
    wanted = neighbour_ids.reshape(wanted_count)
    holder_list = wanted // held_count
    held_entry = wanted % held_count
    rank_list = ranks(holder_list)
    slot_index = holder_list * capacity + rank_list
    slot_cells = jnp.arange(holders_all * capacity, dtype=jnp.int32)
    matches = slot_index[:, None] == slot_cells[None, :]
    request_table = jnp.sum(jnp.where(matches, held_entry[:, None] + 1, 0), axis=0) - 1
    asked = lax.all_to_all(
        request_table.reshape(holders_all, capacity), "db", split_axis=0, concat_axis=0, tiled=True
    )
    flat_keys, flat_values = fetch_slots(
        asked, cache_keys, cache_values, slot_index, holders_all, capacity
    )
    own_keys = flat_keys.reshape(spans_here, 2 * entry_rows, kv_heads, HD)
    own_values = flat_values.reshape(spans_here, 2 * entry_rows, kv_heads, HD)
    block_shape = (spans_here, SPAN, kv_heads, GROUP, HD)
    incoming = shifted_2(jnp.stack([own_keys[-1], own_values[-1]]), "db", 1)
    used_keys = jnp.concatenate([incoming[0][None], own_keys[:-1]], axis=0)
    used_values = jnp.concatenate([incoming[1][None], own_values[:-1]], axis=0)
    empty_row = jnp.zeros((1, row_width), queries.dtype)
    query_rows = jnp.concatenate([empty_row, queries[:-1]], axis=0).reshape(block_shape)
    grad_rows = jnp.concatenate([empty_row, out_grad[:-1]], axis=0).reshape(block_shape)
    local_token = jnp.arange(tokens_here, dtype=jnp.int32) - 1
    global_token = my_index * tokens_here + local_token
    valid_rows = (
        (local_token >= 0)
        & (global_token >= SPAN - 1)
        & ((global_token + half_shift) % LENGTH >= SPAN - 1)
    )
    shifted = attend_blocks(
        query_rows, grad_rows, used_keys, used_values, valid_rows.reshape(spans_here, SPAN)
    ).reshape(tokens_here, row_width)
    last_query = queries[-1:].reshape(1, 1, kv_heads, GROUP, HD)
    last_grad = out_grad[-1:].reshape(1, 1, kv_heads, GROUP, HD)
    last_valid = jnp.ones((1, 1), jnp.bool_)
    last_row = attend(last_query, last_grad, own_keys[-1:], own_values[-1:], last_valid)
    return jnp.concatenate([shifted[1:], last_row.reshape(1, row_width)], axis=0)


def solution(mesh):
    return jax.shard_map(
        body,
        mesh=mesh,
        in_specs=(
            P("db", "heads"),
            P("db", None),
            P("db", None, "heads"),
            P("db", None, "heads"),
            P("db", "heads"),
        ),
        out_specs=P("db", "heads"),
        check_vma=False,
    )
```

profile of v0, /device:TPU:84, one launch (start us, length us, event | category | flops | bytes accessed | tf_op | source)
XLA Modules:
  0.0 312.8 jit_solution(14141962291629935271)
XLA Ops:
  0.0 0.7 broadcast_divide_fusion
  0.7 0.7 sign_compare_fusion
  1.4 0.1 copy.24
  1.5 0.1 div.44
  1.6 0.1 copy.23
  1.7 0.1 rem.54
  1.7 0.1 copy.22
  1.8 0.1 ne.70
  1.9 0.2 convert_reduce_fusion
  2.1 0.1 select_reduce_fusion
  2.2 0.1 sub.62
  2.4 24.7 %all_to_all.16 = s32[64,1,2]{2,1,0:T(1,128)S(1)} all-to-all(s32[64,1,2]{2,1,0:T(1,128)S(1)} %bitcast.183), channel_id=1, replica_groups=mesh['db'=64,'heads'=8] {'db'}, dimensions={0} | all-to-all | bytes 1024 | tf_op jit(solution)/shard_map/all_to_all | solution.py:118
  27.1 0.1 maximum_reduce_fusion
  27.2 0.1 max.12
  27.4 0.0 copy-start.1
  27.4 3.0 gather_fusion
  30.4 3.1 gather_fusion.2
  33.5 5.3 %broadcast_select_fusion = (bf16[128,128,128]{2,1,0:T(8,128)(2,1)}, bf16[128,128,128]{2,1,0:T(8,128)(2,1)S(1)}) fusion(bf16[128,128,128]{2,1,0:T(8,128)(2,1)} %gather_fusion.2, pred[128]{0:T(512)(128)(4,1)S(1)} %compare_and_fusion.1, bf16[128,128,128]{2,1,0:T(8,128)(2,1)} %gather_fusion), kind=kLoop, calls=%fused_computation.4 | loop fusion | flops 4194304 | bytes 16777344 | tf_op jit(solution)/shard_map/jit(_take)/select_n | solution.py:81
  38.8 101.6 %all_to_all.17 = bf16[64,2,128,128]{3,2,1,0:T(8,128)(2,1)} all-to-all(bf16[64,2,128,128]{3,2,1,0:T(8,128)(2,1)S(1)} %bitcast.167), channel_id=1, replica_groups=mesh['db'=64,'heads'=8] {'db'}, dimensions={0} | all-to-all | bytes 8388608 | tf_op jit(solution)/shard_map/all_to_all | solution.py:85
  140.4 19.9 %all-to-all-start.2 = ((bf16[64,2,128,128]{3,2,1,0:T(8,128)(2,1)}), bf16[64,2,128,128]{3,2,1,0:T(8,128)(2,1)}, u32[]{:S(2)}, u32[]{:S(2)}) async-start(bf16[64,2,128,128]{3,2,1,0:T(8,128)(2,1)} %bitcast.166), calls=%async_computation.2 | async-start | bytes 8388608 | tf_op jit(solution)/shard_map/all_to_all | solution.py:86
  160.3 0.0 copy-start.6
  160.3 0.1 concatenate.16
  160.4 0.1 reshape.271
  160.6 0.8 copy-done.6
  161.3 0.1 concatenate.18
  161.4 0.1 reshape.273
  161.6 1.1 bitcast_convert_fusion
  162.7 2.8 gather_fusion.1
  165.6 130.9 %all-to-all-done.2 = bf16[64,2,128,128]{3,2,1,0:T(8,128)(2,1)} async-done(((bf16[64,2,128,128]{3,2,1,0:T(8,128)(2,1)}), bf16[64,2,128,128]{3,2,1,0:T(8,128)(2,1)}, u32[]{:S(2)}, u32[]{:S(2)}) %all-to-all-start.2) | async-done | bytes 4194336 | tf_op jit(solution)/shard_map/all_to_all | solution.py:86
  296.5 2.8 gather_fusion.3
  299.4 0.2 broadcast_select_fusion.2
  299.6 1.9 collective-permute-start
  301.5 0.3 fusion.53
  301.8 0.2 fusion.36
  302.0 0.3 fusion.19
  302.3 0.8 slice.75
  303.1 0.2 fusion.20
  303.4 3.1 collective-permute-done
  306.5 0.5 bitcast_reduce_fusion
  306.9 0.5 fusion.3
  307.5 0.2 copy-done.2
  307.7 0.1 copy-done.3
  307.8 1.0 fusion.10
  308.8 1.7 fusion.6
  310.5 1.3 copy.28
  311.9 0.1 copy.54
  311.9 0.1 slice.76
  312.0 0.8 pad_maximum_fusion
  (26 shorter events, 0.2 us)
Async XLA Ops:
  0.0 27.4 %copy-start = (bf16[6,128,128]{2,1,0:T(8,128)(2,1)S(1)}, bf16[6,128,128]{2,1,0:T(8,128)(2,1)}, u32[]{:S(2)}) copy-start(bf16[6,128,128]{2,1,0:T(8,128)(2,1)} %param.11) | copy-start | bytes 589828
  27.4 3.0 copy-start.1
  140.4 20.0 %copy-start.5 = (bf16[512,384]{1,0:T(8,128)(2,1)S(1)}, bf16[512,384]{1,0:T(8,128)(2,1)}, u32[]{:S(2)}) copy-start(bf16[512,384]{1,0:T(8,128)(2,1)} %param.9) | copy-start | bytes 1179652
  140.4 156.2 %all-to-all-start.2 = ((bf16[64,2,128,128]{3,2,1,0:T(8,128)(2,1)}), bf16[64,2,128,128]{3,2,1,0:T(8,128)(2,1)}, u32[]{:S(2)}, u32[]{:S(2)}) async-start(bf16[64,2,128,128]{3,2,1,0:T(8,128)(2,1)} %bitcast.166), calls=%async_computation.2 | async-start | bytes 8388608 | tf_op jit(solution)/shard_map/all_to_all | solution.py:86
  160.3 1.0 copy-start.6
  299.6 6.9 %collective-permute-start = (bf16[2,256,1,128]{3,1,0,2:T(8,128)(2,1)S(1)}, bf16[2,256,1,128]{3,1,0,2:T(8,128)(2,1)S(1)}, u32[]{:S(2)}, u32[]{:S(2)}) collective-permute-start(bf16[2,256,1,128]{3,1,0,2:T(8,128)(2,1)S(1)} %pad_maximum_fusion.1), channel_id=1, source_target_pairs={{0,8},{8,16},{16,24},{24,32},{32,40},{40,48},{48,56},{56,64},{64,7... | collective-permute-start | bytes 393224 | tf_op jit(solution)/shard_map/ppermute | solution.py:17
  306.4 1.2 copy-start.2
  306.5 1.3 copy-start.3
  307.8 1.0 copy-start.4
where the time goes:
time: 313 us
  waiting for transfers between devices  134 us (43%)
  blocking collectives  126 us (40%)
  starting transfers between devices  21.9 us (7%)
  local copies, waits for them, and re-layouts  16.4 us (5%)
  other arithmetic  9.98 us (3%)
  matrix products  3.97 us (1%)
    all_to_all x1, waiting for transfers between devices, fetch_slots(): lax.all_to_all(send_values, 'db', split_axis=0, concat_axis=0, tiled=True)  131 us
    all_to_all x1, blocking collectives, fetch_slots(): lax.all_to_all(send_keys, 'db', split_axis=0, concat_axis=0, tiled=True)  102 us
    all_to_all x1, blocking collectives, body(): lax.all_to_all(request_table.reshape(holders_all, capacity), 'db', split_...  24.7 us
    all_to_all x1, starting transfers between devices, fetch_slots(): lax.all_to_all(send_values, 'db', split_axis=0, concat_axis=0, tiled=True)  19.9 us
  transfers between devices with their start and end apart: 2, of which 2 were waited for; matrix products, arithmetic and copies ran while one was open for 2% of the time, Pallas kernels for 0%

commit v1 on v0

v1 whole, which is shorter than its diff:
```python
import math

import jax
import jax.numpy as jnp
from jax import lax
from jax.experimental import pallas as pl
from jax.experimental.pallas import tpu as pltpu
from jax.sharding import PartitionSpec as P

HD = 128
GROUP = 3
SPAN = 64
LENGTH = 4096
TAIL = 16


def pack_kernel(ids_ref, keys_ref, values_ref, out_ref):
    entries, pieces = keys_ref.shape[:2]
    holders, chunks, piece, channels = out_ref.shape
    spans = ids_ref.shape[0]
    lane = lax.broadcasted_iota(jnp.int32, (piece, channels), 1)
    places = jnp.zeros((piece, channels), jnp.int32)
    for c in range(2 * spans):
        wanted_id = ids_ref[c // 2, c % 2]
        place = (wanted_id // entries) * chunks + wanted_id % entries - holders * chunks // 2
        places = jnp.where(lane == c, place, places)
    places = places.astype(jnp.float32).astype(jnp.bfloat16)
    for e in range(entries):
        out_ref[0:pieces, e] = keys_ref[e]
        out_ref[pieces : 2 * pieces, e] = values_ref[e]
    out_ref[:, entries] = jnp.broadcast_to(places[None], (holders, piece, channels))


def pick_kernel(index_ref, table_ref, out_ref):
    dests, slots = out_ref.shape[:2]
    wanted = slots - 2

    def one_dest(d, carry):
        for c in range(slots):
            out_ref[d, c] = table_ref[index_ref[d * wanted + c]]
        return carry

    lax.fori_loop(0, dests, one_dest, 0)


def attend(query_rows, grad_rows, keys, values):
    factor = 1.0 / math.sqrt(HD)
    contract = (((1,), (1,)), ((), ()))
    scores = (
        lax.dot_general(query_rows, keys, contract, preferred_element_type=jnp.float32) * factor
    )
    along = lax.dot_general(grad_rows, values, contract, preferred_element_type=jnp.float32)
    expo = jnp.exp(scores - jnp.max(scores, axis=-1, keepdims=True))
    probs = expo / jnp.sum(expo, axis=-1, keepdims=True)
    delta = jnp.sum(probs * along, axis=-1, keepdims=True)
    slope = (probs * (along - delta)).astype(jnp.bfloat16)
    return jnp.dot(slope, keys, preferred_element_type=jnp.float32) * factor


def attend_kernel(start_ref, query_ref, grad_ref, rows_ref, out_ref):
    tokens = query_ref.shape[0]
    blocks = tokens // SPAN
    pieces = rows_ref.shape[0] // 2
    half_shift = tokens // 2
    start = start_ref[0]

    def stacked(ref, parts):
        return jnp.concatenate(
            [ref[a:b, g * HD : (g + 1) * HD] for g in range(GROUP) for a, b in parts], axis=0
        )

    held = None
    for k in range(-1, blocks):
        keys = rows_ref[0:pieces, k + 1].reshape(pieces * 8, HD)
        values = rows_ref[pieces : 2 * pieces, k + 1].reshape(pieces * 8, HD)
        parts = []
        if k >= 0:
            parts.append(((k + 1) * SPAN - TAIL, (k + 1) * SPAN))
        if k + 1 < blocks:
            parts.append(((k + 1) * SPAN, (k + 2) * SPAN))
        result = attend(stacked(query_ref, parts), stacked(grad_ref, parts), keys, values)
        height = sum(b - a for a, b in parts)
        by_head = [result[g * height : (g + 1) * height] for g in range(GROUP)]
        if k >= 0:
            last = lax.broadcasted_iota(jnp.int32, (SPAN, HD), 0) == SPAN - 1
            token = start + k * SPAN + lax.broadcasted_iota(jnp.int32, (SPAN, HD), 0)
            valid = (token >= SPAN - 1) & ((token + half_shift) % LENGTH >= SPAN - 1)
            for g in range(GROUP):
                tail = by_head[g][:TAIL]
                here = jnp.concatenate([held[g][: SPAN - TAIL], jnp.where(last[SPAN - TAIL :], tail, held[g][SPAN - TAIL :])], axis=0)
                out_ref[k * SPAN : (k + 1) * SPAN, g * HD : (g + 1) * HD] = jnp.where(
                    valid, here, 0.0
                ).astype(out_ref.dtype)
        held = [r[TAIL if k >= 0 else 0 :] for r in by_head]


def body(queries, neighbour_ids, cache_keys, cache_values, out_grad):
    holders = lax.axis_size("db")
    me = lax.axis_index("db")
    entries, entry_rows, channels = cache_keys.shape
    tokens, width = queries.shape
    spans = neighbour_ids.shape[0]
    wanted = 2 * spans
    pieces = holders // 2
    piece = entry_rows // pieces
    chunks = entries + 1
    middle = holders * chunks // 2
    vmem = pl.BlockSpec(memory_space=pltpu.VMEM)
    smem = pl.BlockSpec(memory_space=pltpu.SMEM)
    small = pltpu.CompilerParams(vmem_limit_bytes=16 * 2**20)

    packed = pl.pallas_call(
        pack_kernel,
        out_shape=jax.ShapeDtypeStruct((holders, chunks, piece, channels), jnp.bfloat16),
        in_specs=[smem, vmem, vmem],
        out_specs=vmem,
        compiler_params=small,
    )(
        neighbour_ids,
        cache_keys.reshape(entries, pieces, piece, channels),
        cache_values.reshape(entries, pieces, piece, channels),
    )
    spread = lax.all_to_all(packed, "db", split_axis=0, concat_axis=0, tiled=True)
    places = spread[:, entries, 0, :wanted].astype(jnp.int32).reshape(holders * wanted) + middle
    places = jnp.concatenate([jnp.zeros((2,), jnp.int32), places])
    picked = pl.pallas_call(
        pick_kernel,
        out_shape=jax.ShapeDtypeStruct((holders, wanted + 2, piece, channels), jnp.bfloat16),
        in_specs=[smem, vmem],
        out_specs=vmem,
        compiler_params=small,
    )(places, spread.reshape(holders * chunks, piece, channels))
    arrived = lax.all_to_all(
        picked.reshape(holders, (wanted + 2) * piece, channels),
        "db", split_axis=0, concat_axis=0, tiled=True,
    ).reshape(holders, spans + 1, 2 * piece, channels)
    return pl.pallas_call(
        attend_kernel,
        out_shape=jax.ShapeDtypeStruct((tokens, width), jnp.bfloat16),
        in_specs=[smem] + [vmem] * 3,
        out_specs=vmem,
        compiler_params=small,
    )((me * tokens).reshape(1).astype(jnp.int32), queries, out_grad, arrived)


def solution(mesh):
    return jax.shard_map(
        body,
        mesh=mesh,
        in_specs=(
            P("db", "heads"),
            P("db", None),
            P("db", None, "heads"),
            P("db", None, "heads"),
            P("db", "heads"),
        ),
        out_specs=P("db", "heads"),
        check_vma=False,
    )
```

time: 313 us -> 83.1 us (0.27)
  the two profiles are of different devices: /device:TPU:84 before, /device:TPU:6 now
where the time goes in v1:
time: 83.1 us; the launch traced here: 82.3 us
  blocking collectives  34.5 us (42%)
  waiting for transfers between devices  31.9 us (38%)
  Pallas kernels  7.66 us (9%)
  starting transfers between devices  5.28 us (6%)
  local copies, waits for them, and re-layouts  2.76 us (3%)
    all_to_all x1, blocking collectives, body(): lax.all_to_all(packed, 'db', split_axis=0, concat_axis=0, tiled=True)  34.5 us
    all_to_all x1, waiting for transfers between devices, body(): lax.all_to_all(picked.reshape(holders, (wanted + 2) * piece, channels), '...  31.9 us
    all_to_all x1, starting transfers between devices, body(): lax.all_to_all(picked.reshape(holders, (wanted + 2) * piece, channels), '...  5.28 us
    pallas_call x1, Pallas kernels, body(): pl.pallas_call(attend_kernel, out_shape=jax.ShapeDtypeStruct((tokens, wid...  3.65 us
    pallas_call x1, Pallas kernels, body(): pl.pallas_call(pick_kernel, out_shape=jax.ShapeDtypeStruct((holders, want...  3.14 us
    unnamed x9, local copies, waits for them, and re-layouts  2.61 us
  transfers between devices with their start and end apart: 1, of which 1 were waited for; matrix products, arithmetic and copies ran while one was open for 0% of the time, Pallas kernels for 0%

profile of v1, /device:TPU:6, one launch (start us, length us, event | category | flops | bytes accessed | tf_op | source)
XLA Modules:
  0.0 82.3 jit_solution(17168522090625522247)
XLA Ops:
  0.0 0.8 copy.7.ids_ref
  0.8 0.0 copy-start.2
  0.8 0.9 %copy-done.2 = bf16[6,128,128]{2,1,0:T(8,128)(2,1)S(1)} copy-done((bf16[6,128,128]{2,1,0:T(8,128)(2,1)S(1)}, bf16[6,128,128]{2,1,0:T(8,128)(2,1)}, u32[]{:S(2)}) %copy-start.2) | copy-done | bytes 196632
  1.7 0.0 copy-start.3
  1.7 0.9 %copy-done.3 = bf16[6,128,128]{2,1,0:T(8,128)(2,1)S(1)} copy-done((bf16[6,128,128]{2,1,0:T(8,128)(2,1)S(1)}, bf16[6,128,128]{2,1,0:T(8,128)(2,1)}, u32[]{:S(2)}) %copy-start.3) | copy-done | bytes 196632
  2.6 0.9 %shard_map.55 = bf16[64,7,4,128]{3,2,1,0:T(4,128)(2,1)S(1)} custom-call(s32[8,2]{1,0:T(8,128)S(1)} %copy.7.ids_ref, bf16[6,32,4,128]{3,2,1,0:T(4,128)(2,1)S(1)} %bitcast.8, bf16[6,32,4,128]{3,2,1,0:T(4,128)(2,1)S(1)} %bitcast.9), custom_call_target="tpu_custom_call" | custom-call | tf_op jit(solution)/shard_map/pallas_call | solution.py:112
  3.5 34.5 %all_to_all.10 = bf16[64,7,4,128]{3,2,1,0:T(4,128)(2,1)S(1)} all-to-all(bf16[64,7,4,128]{3,2,1,0:T(4,128)(2,1)S(1)} %shard_map.55), channel_id=1, replica_groups=mesh['db'=64,'heads'=8] {'db'}, dimensions={0} | all-to-all | bytes 917504 | tf_op jit(solution)/shard_map/all_to_all | solution.py:123
  38.0 0.1 fusion.1
  38.1 0.1 add.13
  38.2 0.1 concatenate.3.index_ref
  38.3 3.1 %shard_map.56 = bf16[64,18,4,128]{3,2,1,0:T(4,128)(2,1)} custom-call(s32[1026]{0:T(1024)S(1)} %concatenate.3.index_ref, bf16[448,4,128]{2,1,0:T(4,128)(2,1)S(1)} %bitcast.7), custom_call_target="tpu_custom_call" | custom-call | tf_op jit(solution)/shard_map/pallas_call | solution.py:126
  41.4 0.0 copy-start
  41.4 0.0 copy-start.1
  41.4 5.3 %all-to-all-start.1 = ((bf16[64,72,128]{2,1,0:T(8,128)(2,1)}), bf16[64,72,128]{2,1,0:T(8,128)(2,1)S(1)}, u32[]{:S(2)}, u32[]{:S(2)}) async-start(bf16[64,72,128]{2,1,0:T(8,128)(2,1)} %bitcast.4), calls=%async_computation.1 | async-start | bytes 2359296 | tf_op jit(solution)/shard_map/all_to_all | solution.py:133
  46.7 31.9 %all-to-all-done.1 = bf16[64,72,128]{2,1,0:T(8,128)(2,1)S(1)} async-done(((bf16[64,72,128]{2,1,0:T(8,128)(2,1)}), bf16[64,72,128]{2,1,0:T(8,128)(2,1)S(1)}, u32[]{:S(2)}, u32[]{:S(2)}) %all-to-all-start.1) | async-done | bytes 1179680 | tf_op jit(solution)/shard_map/all_to_all | solution.py:133
  78.6 0.0 copy-done
  78.6 0.0 copy-done.1
  78.6 3.7 %shard_map.57 = bf16[512,384]{1,0:T(8,128)(2,1)} custom-call(s32[1]{0:T(128)} %bitcast.start_ref, bf16[512,384]{1,0:T(8,128)(2,1)S(1)} %copy-done, bf16[512,384]{1,0:T(8,128)(2,1)S(1)} %copy-done.1, bf16[64,9,8,128]{3,2,1,0:T(8,128)(2,1)S(1)} %bitcast.6), custom_call_target="tpu_custom_call" | custom-call | tf_op jit(solution)/shard_map/pallas_call | solution.py:137
Async XLA Ops:
  0.8 0.9 %copy-start.2 = (bf16[6,128,128]{2,1,0:T(8,128)(2,1)S(1)}, bf16[6,128,128]{2,1,0:T(8,128)(2,1)}, u32[]{:S(2)}) copy-start(bf16[6,128,128]{2,1,0:T(8,128)(2,1)} %param.7) | copy-start | bytes 589828
  1.7 0.9 %copy-start.3 = (bf16[6,128,128]{2,1,0:T(8,128)(2,1)S(1)}, bf16[6,128,128]{2,1,0:T(8,128)(2,1)}, u32[]{:S(2)}) copy-start(bf16[6,128,128]{2,1,0:T(8,128)(2,1)} %param.8) | copy-start | bytes 589828
  41.4 37.2 %copy-start = (bf16[512,384]{1,0:T(8,128)(2,1)S(1)}, bf16[512,384]{1,0:T(8,128)(2,1)}, u32[]{:S(2)}) copy-start(bf16[512,384]{1,0:T(8,128)(2,1)} %query_ref.1) | copy-start | bytes 1179652
  41.4 37.2 %copy-start.1 = (bf16[512,384]{1,0:T(8,128)(2,1)S(1)}, bf16[512,384]{1,0:T(8,128)(2,1)}, u32[]{:S(2)}) copy-start(bf16[512,384]{1,0:T(8,128)(2,1)} %grad_ref.1) | copy-start | bytes 1179652
  41.4 37.2 %all-to-all-start.1 = ((bf16[64,72,128]{2,1,0:T(8,128)(2,1)}), bf16[64,72,128]{2,1,0:T(8,128)(2,1)S(1)}, u32[]{:S(2)}, u32[]{:S(2)}) async-start(bf16[64,72,128]{2,1,0:T(8,128)(2,1)} %bitcast.4), calls=%async_computation.1 | async-start | bytes 2359296 | tf_op jit(solution)/shard_map/all_to_all | solution.py:133

commit v2 on v1

v2 whole, which is shorter than its diff:
```python
import math

import jax
import jax.numpy as jnp
from jax import lax
from jax.experimental import pallas as pl
from jax.experimental.pallas import tpu as pltpu
from jax.sharding import PartitionSpec as P

HD = 128
GROUP = 3
SPAN = 64
LENGTH = 4096
TAIL = 16
CHUNK = 192


def pack_kernel(ids_ref, keys_ref, values_ref, out_ref, sems):
    entries, pieces = keys_ref.shape[:2]
    holders, chunks, piece, channels = out_ref.shape
    spans = ids_ref.shape[1]
    copies = []
    for e in range(entries):
        for n, ref in enumerate((keys_ref, values_ref)):
            copies.append(
                pltpu.make_async_copy(
                    ref.at[e], out_ref.at[pl.ds(n * pieces, pieces), e], sems.at[n, e]
                )
            )
    for copy in copies:
        copy.start()
    lane = lax.broadcasted_iota(jnp.int32, (piece, channels), 1)
    places = jnp.zeros((piece, channels), jnp.int32)
    for c in range(2 * spans):
        wanted_id = ids_ref[c % 2, c // 2]
        place = (wanted_id // entries) * chunks + wanted_id % entries - holders * chunks // 2
        places = jnp.where(lane == c, place, places)
    places = places.astype(jnp.float32).astype(jnp.bfloat16)
    out_ref[:, entries] = jnp.broadcast_to(places[None], (holders, piece, channels))
    for copy in copies:
        copy.wait()


def pick_kernel(index_ref, table_ref, out_ref, buffer_ref, sems):
    dests, slots = out_ref.shape[0], out_ref.shape[1] // 2
    wanted = slots - 2
    parts = sems.shape[0]
    copies = []
    for part in range(parts):
        here = pl.ds(part * (dests // parts), dests // parts)
        for d in range(here.start, here.start + here.size):
            for c in range(slots):
                buffer_ref[d, 2 * c : 2 * c + 2] = table_ref[
                    pl.ds(index_ref[d * wanted + c], 2)
                ]
        copies.append(
            pltpu.make_async_copy(buffer_ref.at[here], out_ref.at[here], sems.at[part])
        )
        copies[-1].start()
    for copy in copies:
        copy.wait()


def shift_kernel(query_ref, grad_ref, query_out_ref, grad_out_ref, wide_ref):
    tokens, width = query_ref.shape
    blocks = tokens // SPAN
    wide_ref[0:8] = jnp.zeros((8, width), jnp.float32)
    wide_ref[tokens + 8 :] = jnp.zeros((SPAN, width), jnp.float32)
    for ref, out_ref in ((query_ref, query_out_ref), (grad_ref, grad_out_ref)):
        wide_ref[8 : tokens + 8] = ref[...].astype(jnp.float32)
        for n in range(blocks + 1):
            for g in range(GROUP):
                out_ref[n, g * SPAN : (g + 1) * SPAN] = wide_ref[
                    7 + n * SPAN : 7 + (n + 1) * SPAN, g * HD : (g + 1) * HD
                ].astype(out_ref.dtype)


def soften(scores, along):
    factor = 1.0 / math.sqrt(HD)
    highest = jnp.max(scores, axis=-1, keepdims=True)
    expo = jnp.exp2((scores - highest) * (factor / math.log(2.0)))
    scale = 1.0 / jnp.sum(expo, axis=-1, keepdims=True)
    delta = jnp.sum(expo * along, axis=-1, keepdims=True) * scale
    return (expo * (along - delta)).astype(jnp.bfloat16), scale * factor


def attend_kernel(start_ref, query_ref, grad_ref, rows_ref, out_ref, result_ref, scores_ref, along_ref, slope_ref, scale_ref, sems):
    tokens = out_ref.shape[0]
    blocks = tokens // SPAN
    pieces = rows_ref.shape[0] // 2
    half_shift = tokens // 2
    start = start_ref[0]
    row = lax.broadcasted_iota(jnp.int32, (SPAN, HD), 0)
    contract = (((1,), (1,)), ((), ()))

    def height(n):
        return SPAN if n < blocks else TAIL

    def keys_of(n):
        return rows_ref[0:pieces, n].reshape(pieces * 8, HD)

    def products(n):
        values = rows_ref[pieces : 2 * pieces, n].reshape(pieces * 8, HD)
        for ref, other, out in ((query_ref, keys_of(n), scores_ref), (grad_ref, values, along_ref)):
            if n < blocks:
                rows = ref[n]
            else:
                rows = jnp.concatenate(
                    [ref[n, g * SPAN : g * SPAN + TAIL] for g in range(GROUP)], axis=0
                )
            out[n % 2, : GROUP * height(n)] = lax.dot_general(
                rows, other, contract, preferred_element_type=jnp.float32
            )

    held, copies = None, []
    products(0)
    for n in range(blocks + 1):
        if n < blocks:
            products(n + 1)
        total = GROUP * height(n)
        step = min(CHUNK, total)
        for at in range(0, total, step):
            here = slice(at, at + step)
            slope, scale = soften(scores_ref[n % 2, here], along_ref[n % 2, here])
            slope_ref[n % 2, here] = slope
            scale_ref[n % 2, here] = jnp.broadcast_to(scale, (step, HD))
        result = (
            jnp.dot(slope_ref[n % 2, :total], keys_of(n), preferred_element_type=jnp.float32)
            * scale_ref[n % 2, :total]
        )
        turned = [
            pltpu.roll(result[g * height(n) : (g + 1) * height(n)], height(n) - 1, 0)
            for g in range(GROUP)
        ]
        if n > 0:
            token = start + (n - 1) * SPAN + row
            valid = (token >= SPAN - 1) & ((token + half_shift) % LENGTH >= SPAN - 1)
            for g in range(GROUP):
                end = jnp.where(row[-8:] == SPAN - 1, turned[g][-8:], held[g][-8:])
                here = jnp.concatenate([held[g][:-8], end], axis=0)
                result_ref[(n - 1) * SPAN : n * SPAN, g * HD : (g + 1) * HD] = jnp.where(
                    valid, here, 0.0
                ).astype(out_ref.dtype)
            rows = pl.ds((n - 1) * SPAN, SPAN)
            copies.append(
                pltpu.make_async_copy(result_ref.at[rows], out_ref.at[rows], sems.at[n - 1])
            )
            copies[-1].start()
        held = turned
    for copy in copies:
        copy.wait()


def body(queries, neighbour_ids, cache_keys, cache_values, out_grad):
    holders = lax.axis_size("db")
    me = lax.axis_index("db")
    entries, entry_rows, channels = cache_keys.shape
    tokens, width = queries.shape
    spans = neighbour_ids.shape[0]
    wanted = 2 * spans
    pieces = holders // 2
    piece = entry_rows // pieces
    chunks = entries + 1
    middle = holders * chunks // 2
    vmem = pl.BlockSpec(memory_space=pltpu.VMEM)
    smem = pl.BlockSpec(memory_space=pltpu.SMEM)
    hbm = pl.BlockSpec(memory_space=pltpu.HBM)
    small = pltpu.CompilerParams(vmem_limit_bytes=16 * 2**20)

    packed = pl.pallas_call(
        pack_kernel,
        out_shape=jax.ShapeDtypeStruct((holders, chunks, piece, channels), jnp.bfloat16),
        in_specs=[smem, hbm, hbm],
        out_specs=vmem,
        scratch_shapes=[pltpu.SemaphoreType.DMA((2, entries))],
        compiler_params=small,
    )(
        neighbour_ids.T,
        *(
            pltpu.with_memory_space_constraint(
                x.reshape(entries, pieces, piece, channels), pltpu.HBM
            )
            for x in (cache_keys, cache_values)
        ),
    )
    spread = lax.all_to_all(packed, "db", split_axis=0, concat_axis=0, tiled=True)
    places = (spread[:, entries, 0, :wanted].astype(jnp.int32) + middle) * 2
    places = places.reshape(holders * wanted)
    places = jnp.concatenate([jnp.zeros((2,), jnp.int32), places])
    picked = pl.pallas_call(
        pick_kernel,
        out_shape=jax.ShapeDtypeStruct((holders, 2 * (wanted + 2), piece // 2, channels), jnp.bfloat16),
        in_specs=[smem, vmem],
        out_specs=hbm,
        scratch_shapes=[
            pltpu.VMEM((holders, 2 * (wanted + 2), piece // 2, channels), jnp.bfloat16),
            pltpu.SemaphoreType.DMA((4,)),
        ],
        compiler_params=small,
    )(places, spread.reshape(holders * chunks * 2, piece // 2, channels))
    arrived = lax.all_to_all(
        picked.reshape(holders, (wanted + 2) * piece, channels),
        "db", split_axis=0, concat_axis=0, tiled=True,
    ).reshape(holders, spans + 1, 2 * piece, channels)
    stacked = jax.ShapeDtypeStruct((spans + 1, GROUP * SPAN, HD), jnp.bfloat16)
    query_rows, grad_rows = pl.pallas_call(
        shift_kernel,
        out_shape=(stacked, stacked),
        in_specs=[vmem] * 2,
        out_specs=(vmem, vmem),
        scratch_shapes=[pltpu.VMEM((tokens + 8 + SPAN, width), jnp.float32)],
        compiler_params=small,
        cost_estimate=pl.CostEstimate(flops=10**6, bytes_accessed=4 * 10**6, transcendentals=0),
    )(queries, out_grad)
    return pl.pallas_call(
        attend_kernel,
        out_shape=jax.ShapeDtypeStruct((tokens, width), jnp.bfloat16),
        in_specs=[smem] + [vmem] * 3,
        out_specs=hbm,
        scratch_shapes=[
            pltpu.VMEM((tokens, width), jnp.bfloat16),
            pltpu.VMEM((2, GROUP * SPAN, 2 * entry_rows), jnp.float32),
            pltpu.VMEM((2, GROUP * SPAN, 2 * entry_rows), jnp.float32),
            pltpu.VMEM((2, GROUP * SPAN, 2 * entry_rows), jnp.bfloat16),
            pltpu.VMEM((2, GROUP * SPAN, HD), jnp.float32),
            pltpu.SemaphoreType.DMA((spans,)),
        ],
        compiler_params=small,
    )((me * tokens).reshape(1).astype(jnp.int32), query_rows, grad_rows, arrived)


def solution(mesh):
    return jax.shard_map(
        body,
        mesh=mesh,
        in_specs=(
            P("db", "heads"),
            P("db", None),
            P("db", None, "heads"),
            P("db", None, "heads"),
            P("db", "heads"),
        ),
        out_specs=P("db", "heads"),
        check_vma=False,
    )
```

time: 83.1 us -> 79.5 us (0.957)
  local copies, waits for them, and re-layouts: 2.76 us -> 0.84 us
  Pallas kernels: 7.66 us -> 6.41 us
    unnamed x9 -> x6, local copies, waits for them, and re-layouts: 2.61 us -> 0.69 us
    pallas_call x1, Pallas kernels: 3.65 us -> 2.35 us  [body(): pl.pallas_call(attend_kernel, out_shape=jax.ShapeDtypeStruct((tokens, wid...]
    pallas_call x1 -> x2, Pallas kernels: 3.14 us -> 2.47 us  [the longest x1 1.96 us: body(): pl.pallas_call(pick_kernel, out_shape=jax.ShapeDtypeStruct((holders, 2 *...]
  transfers between devices with their start and end apart: 1 -> 1, of which waited for: 1 -> 1; matrix products, arithmetic and copies ran while one was open for 0% -> 0% of each run, Pallas kernels for 0% -> 1%
where the time goes in v2:
time: 79.5 us; the launch traced here: 78.6 us
  blocking collectives  34.5 us (43%)
  waiting for transfers between devices  31.4 us (39%)
  Pallas kernels  6.41 us (8%)
  starting transfers between devices  5.29 us (7%)
  local copies, waits for them, and re-layouts  0.84 us (1%)
    all_to_all x1, blocking collectives, body(): lax.all_to_all(packed, 'db', split_axis=0, concat_axis=0, tiled=True)  34.5 us
    all_to_all x1, waiting for transfers between devices, body(): lax.all_to_all(picked.reshape(holders, (wanted + 2) * piece, channels), '...  31.4 us
    all_to_all x1, starting transfers between devices, body(): lax.all_to_all(picked.reshape(holders, (wanted + 2) * piece, channels), '...  5.29 us
    pallas_call x1, Pallas kernels, body(): pl.pallas_call(attend_kernel, out_shape=jax.ShapeDtypeStruct((tokens, wid...  2.35 us
    pallas_call x1, Pallas kernels, body(): pl.pallas_call(pick_kernel, out_shape=jax.ShapeDtypeStruct((holders, 2 *...  1.96 us
  transfers between devices with their start and end apart: 1, of which 1 were waited for; matrix products, arithmetic and copies ran while one was open for 0% of the time, Pallas kernels for 1%

profile of v2, /device:TPU:6, one launch (start us, length us, event | category | flops | bytes accessed | tf_op | source)
XLA Modules:
  0.0 78.6 jit_solution(9542825277430971876)
XLA Ops:
  0.0 0.0 copy-start.2
  0.0 0.7 copy-done.2
  0.7 1.6 %shard_map.56 = bf16[64,7,4,128]{3,2,1,0:T(4,128)(2,1)S(1)} custom-call(s32[2,8]{1,0:T(2,128)S(1)} %bitcast.9, bf16[6,32,4,128]{3,2,1,0:T(4,128)(2,1)} %bitcast.10, bf16[6,32,4,128]{3,2,1,0:T(4,128)(2,1)} %bitcast.11), custom_call_target="tpu_custom_call" | custom-call | tf_op jit(solution)/shard_map/pallas_call | solution.py:170
  2.3 34.5 %all_to_all.10 = bf16[64,7,4,128]{3,2,1,0:T(4,128)(2,1)S(1)} all-to-all(bf16[64,7,4,128]{3,2,1,0:T(4,128)(2,1)S(1)} %shard_map.56), channel_id=1, replica_groups=mesh['db'=64,'heads'=8] {'db'}, dimensions={0} | all-to-all | bytes 917504 | tf_op jit(solution)/shard_map/all_to_all | solution.py:186
  36.8 0.1 fusion.2
  36.9 0.1 mul.16
  37.0 0.1 concatenate.3.index_ref
  37.1 2.0 %shard_map.57 = bf16[64,36,2,128]{3,2,1,0:T(2,128)(2,1)} custom-call(s32[1026]{0:T(1024)S(1)} %concatenate.3.index_ref, bf16[896,2,128]{2,1,0:T(2,128)(2,1)S(1)} %bitcast.8), custom_call_target="tpu_custom_call" | custom-call | tf_op jit(solution)/shard_map/pallas_call | solution.py:190
  39.1 0.0 copy-start
  39.1 0.0 copy-start.1
  39.1 5.3 %all-to-all-start.1 = ((bf16[64,72,128]{2,1,0:T(8,128)(2,1)}), bf16[64,72,128]{2,1,0:T(8,128)(2,1)S(1)}, u32[]{:S(2)}, u32[]{:S(2)}) async-start(bf16[64,72,128]{2,1,0:T(8,128)(2,1)} %bitcast.5), calls=%async_computation.1 | async-start | bytes 2359296 | tf_op jit(solution)/shard_map/all_to_all | solution.py:201
  44.4 0.0 copy-done
  44.4 0.0 copy-done.1
  44.4 0.5 shard_map.55
  44.9 31.4 %all-to-all-done.1 = bf16[64,72,128]{2,1,0:T(8,128)(2,1)S(1)} async-done(((bf16[64,72,128]{2,1,0:T(8,128)(2,1)}), bf16[64,72,128]{2,1,0:T(8,128)(2,1)S(1)}, u32[]{:S(2)}, u32[]{:S(2)}) %all-to-all-start.1) | async-done | bytes 1179680 | tf_op jit(solution)/shard_map/all_to_all | solution.py:201
  76.3 2.4 %shard_map.58 = bf16[512,384]{1,0:T(8,128)(2,1)} custom-call(s32[1]{0:T(128)} %bitcast.start_ref, bf16[9,192,128]{2,1,0:T(8,128)(2,1)S(1)} %get-tuple-element.7.query_ref, bf16[9,192,128]{2,1,0:T(8,128)(2,1)S(1)} %get-tuple-element.8.grad_ref, bf16[64,9,8,128]{3,2,1,0:T(8,128)(2,1)S(1)} %bitcast.7), custom_call_target="tpu_custom_call" | custom-call | tf_op jit(solution)/shard_map/pallas_call | solution.py:215
Async XLA Ops:
  0.0 0.7 copy-start.2
  39.1 5.3 %copy-start = (bf16[512,384]{1,0:T(8,128)(2,1)S(1)}, bf16[512,384]{1,0:T(8,128)(2,1)}, u32[]{:S(2)}) copy-start(bf16[512,384]{1,0:T(8,128)(2,1)} %query_ref.1) | copy-start | bytes 1179652
  39.1 5.3 %copy-start.1 = (bf16[512,384]{1,0:T(8,128)(2,1)S(1)}, bf16[512,384]{1,0:T(8,128)(2,1)}, u32[]{:S(2)}) copy-start(bf16[512,384]{1,0:T(8,128)(2,1)} %grad_ref.1) | copy-start | bytes 1179652
  39.1 37.2 %all-to-all-start.1 = ((bf16[64,72,128]{2,1,0:T(8,128)(2,1)}), bf16[64,72,128]{2,1,0:T(8,128)(2,1)S(1)}, u32[]{:S(2)}, u32[]{:S(2)}) async-start(bf16[64,72,128]{2,1,0:T(8,128)(2,1)} %bitcast.5), calls=%async_computation.1 | async-start | bytes 2359296 | tf_op jit(solution)/shard_map/all_to_all | solution.py:201

commit v3 on v2

--- a/solution.py
+++ b/solution.py
@@ -12,13 +12,18 @@
 SPAN = 64
 LENGTH = 4096
 TAIL = 16
-CHUNK = 192
-
-
-def pack_kernel(ids_ref, keys_ref, values_ref, out_ref, sems):
+AHEAD = 3
+LAG = 2
+SLOTS = AHEAD + LAG + 1
+LAST_AT = 0
+
+
+def pack_kernel(ids_hbm_ref, keys_ref, values_ref, out_ref, ids_ref, sems, ids_sem):
     entries, pieces = keys_ref.shape[:2]
     holders, chunks, piece, channels = out_ref.shape
     spans = ids_ref.shape[1]
+    ids_copy = pltpu.make_async_copy(ids_hbm_ref, ids_ref, ids_sem)
+    ids_copy.start()
     copies = []
     for e in range(entries):
         for n, ref in enumerate((keys_ref, values_ref)):
@@ -29,6 +34,7 @@
             )
     for copy in copies:
         copy.start()
+    ids_copy.wait()
     lane = lax.broadcasted_iota(jnp.int32, (piece, channels), 1)
     places = jnp.zeros((piece, channels), jnp.int32)
     for c in range(2 * spans):
@@ -99,7 +105,7 @@
     def keys_of(n):
         return rows_ref[0:pieces, n].reshape(pieces * 8, HD)
 
-    def products(n):
+    def products(n, slot):
         values = rows_ref[pieces : 2 * pieces, n].reshape(pieces * 8, HD)
         for ref, other, out in ((query_ref, keys_of(n), scores_ref), (grad_ref, values, along_ref)):
             if n < blocks:
@@ -108,45 +114,57 @@
                 rows = jnp.concatenate(
                     [ref[n, g * SPAN : g * SPAN + TAIL] for g in range(GROUP)], axis=0
                 )
-            out[n % 2, : GROUP * height(n)] = lax.dot_general(
+            out[slot, : GROUP * height(n)] = lax.dot_general(
                 rows, other, contract, preferred_element_type=jnp.float32
             )
 
-    held, copies = None, []
-    products(0)
-    for n in range(blocks + 1):
-        if n < blocks:
-            products(n + 1)
+    def softened(n, slot):
         total = GROUP * height(n)
-        step = min(CHUNK, total)
-        for at in range(0, total, step):
-            here = slice(at, at + step)
-            slope, scale = soften(scores_ref[n % 2, here], along_ref[n % 2, here])
-            slope_ref[n % 2, here] = slope
-            scale_ref[n % 2, here] = jnp.broadcast_to(scale, (step, HD))
+        slope, scale = soften(scores_ref[slot, :total], along_ref[slot, :total])
+        slope_ref[slot, :total] = slope
+        scale_ref[slot, :total] = jnp.broadcast_to(scale, (total, HD))
+
+    def finished(n, slot):
+        total = GROUP * height(n)
         result = (
-            jnp.dot(slope_ref[n % 2, :total], keys_of(n), preferred_element_type=jnp.float32)
-            * scale_ref[n % 2, :total]
+            jnp.dot(slope_ref[slot, :total], keys_of(n), preferred_element_type=jnp.float32)
+            * scale_ref[slot, :total]
         )
-        turned = [
+        return [
             pltpu.roll(result[g * height(n) : (g + 1) * height(n)], height(n) - 1, 0)
             for g in range(GROUP)
         ]
-        if n > 0:
-            token = start + (n - 1) * SPAN + row
-            valid = (token >= SPAN - 1) & ((token + half_shift) % LENGTH >= SPAN - 1)
+
+    order = [n for n in range(blocks)]
+    order.insert(LAST_AT, blocks)
+    turned, copies = {}, []
+    for at in range(-AHEAD, len(order) + LAG):
+        if 0 <= at + AHEAD < len(order):
+            products(order[at + AHEAD], (at + AHEAD) % SLOTS)
+        if 0 <= at < len(order):
+            softened(order[at], at % SLOTS)
+        if at < LAG:
+            continue
+        done = order[at - LAG]
+        turned[done] = finished(done, (at - LAG) % SLOTS)
+        for n in range(1, blocks + 1):
+            if done not in (n, n - 1) or n not in turned or n - 1 not in turned:
+                continue
+            token = start + (n - 1) * SPAN
+            idle = (token == 0) | ((token + half_shift) % LENGTH == 0)
+            kept = row >= jnp.where(idle, SPAN - 1, 0)
             for g in range(GROUP):
-                end = jnp.where(row[-8:] == SPAN - 1, turned[g][-8:], held[g][-8:])
-                here = jnp.concatenate([held[g][:-8], end], axis=0)
+                before, after = turned[n - 1][g], turned[n][g]
+                end = jnp.where(row[-8:] == SPAN - 1, after[-8:], before[-8:])
+                here = jnp.concatenate([before[:-8], end], axis=0)
                 result_ref[(n - 1) * SPAN : n * SPAN, g * HD : (g + 1) * HD] = jnp.where(
-                    valid, here, 0.0
+                    kept, here, 0.0
                 ).astype(out_ref.dtype)
             rows = pl.ds((n - 1) * SPAN, SPAN)
             copies.append(
                 pltpu.make_async_copy(result_ref.at[rows], out_ref.at[rows], sems.at[n - 1])
             )
             copies[-1].start()
-        held = turned
     for copy in copies:
         copy.wait()
 
@@ -170,12 +188,16 @@
     packed = pl.pallas_call(
         pack_kernel,
         out_shape=jax.ShapeDtypeStruct((holders, chunks, piece, channels), jnp.bfloat16),
-        in_specs=[smem, hbm, hbm],
+        in_specs=[hbm] * 3,
         out_specs=vmem,
-        scratch_shapes=[pltpu.SemaphoreType.DMA((2, entries))],
+        scratch_shapes=[
+            pltpu.SMEM((2, spans), jnp.int32),
+            pltpu.SemaphoreType.DMA((2, entries)),
+            pltpu.SemaphoreType.DMA,
+        ],
         compiler_params=small,
     )(
-        neighbour_ids.T,
+        pltpu.with_memory_space_constraint(neighbour_ids.T, pltpu.HBM),
         *(
             pltpu.with_memory_space_constraint(
                 x.reshape(entries, pieces, piece, channels), pltpu.HBM
@@ -219,10 +241,10 @@
         out_specs=hbm,
         scratch_shapes=[
             pltpu.VMEM((tokens, width), jnp.bfloat16),
-            pltpu.VMEM((2, GROUP * SPAN, 2 * entry_rows), jnp.float32),
-            pltpu.VMEM((2, GROUP * SPAN, 2 * entry_rows), jnp.float32),
-            pltpu.VMEM((2, GROUP * SPAN, 2 * entry_rows), jnp.bfloat16),
-            pltpu.VMEM((2, GROUP * SPAN, HD), jnp.float32),
+            pltpu.VMEM((SLOTS, GROUP * SPAN, 2 * entry_rows), jnp.float32),
+            pltpu.VMEM((SLOTS, GROUP * SPAN, 2 * entry_rows), jnp.float32),
+            pltpu.VMEM((SLOTS, GROUP * SPAN, 2 * entry_rows), jnp.bfloat16),
+            pltpu.VMEM((SLOTS, GROUP * SPAN, HD), jnp.float32),
             pltpu.SemaphoreType.DMA((spans,)),
         ],
         compiler_params=small,

time: 79.5 us -> 77.8 us (0.979)
  Pallas kernels: 6.41 us -> 5.47 us
where the time goes in v3:
time: 77.8 us; the launch traced here: 77 us
  blocking collectives  34.5 us (44%)
  waiting for transfers between devices  31.4 us (40%)
  Pallas kernels  5.47 us (7%)
  starting transfers between devices  5.29 us (7%)
    all_to_all x1, blocking collectives, body(): lax.all_to_all(packed, 'db', split_axis=0, concat_axis=0, tiled=True)  34.5 us
    all_to_all x1, waiting for transfers between devices, body(): lax.all_to_all(picked.reshape(holders, (wanted + 2) * piece, channels), '...  31.4 us
    all_to_all x1, starting transfers between devices, body(): lax.all_to_all(picked.reshape(holders, (wanted + 2) * piece, channels), '...  5.29 us
    pallas_call x1, Pallas kernels, body(): pl.pallas_call(pick_kernel, out_shape=jax.ShapeDtypeStruct((holders, 2 *...  1.96 us
    pallas_call x1, Pallas kernels, body(): pl.pallas_call(attend_kernel, out_shape=jax.ShapeDtypeStruct((tokens, wid...  1.92 us
  transfers between devices with their start and end apart: 1, of which 1 were waited for; matrix products, arithmetic and copies ran while one was open for 0% of the time, Pallas kernels for 1%

profile of v3, /device:TPU:6, one launch (start us, length us, event | category | flops | bytes accessed | tf_op | source)
XLA Modules:
  0.0 77.0 jit_solution(12125009589972963600)
XLA Ops:
  0.0 1.1 %shard_map.56 = bf16[64,7,4,128]{3,2,1,0:T(4,128)(2,1)S(1)} custom-call(s32[2,8]{1,0:T(2,128)} %bitcast.11, bf16[6,32,4,128]{3,2,1,0:T(4,128)(2,1)} %bitcast.9, bf16[6,32,4,128]{3,2,1,0:T(4,128)(2,1)} %bitcast.10), custom_call_target="tpu_custom_call" | custom-call | tf_op jit(solution)/shard_map/pallas_call | solution.py:188
  1.1 34.5 %all_to_all.10 = bf16[64,7,4,128]{3,2,1,0:T(4,128)(2,1)S(1)} all-to-all(bf16[64,7,4,128]{3,2,1,0:T(4,128)(2,1)S(1)} %shard_map.56), channel_id=1, replica_groups=mesh['db'=64,'heads'=8] {'db'}, dimensions={0} | all-to-all | bytes 917504 | tf_op jit(solution)/shard_map/all_to_all | solution.py:208
  35.6 0.1 fusion.2
  35.8 0.1 mul.16
  35.8 0.1 concatenate.3.index_ref
  35.9 2.0 %shard_map.57 = bf16[64,36,2,128]{3,2,1,0:T(2,128)(2,1)} custom-call(s32[1026]{0:T(1024)S(1)} %concatenate.3.index_ref, bf16[896,2,128]{2,1,0:T(2,128)(2,1)S(1)} %bitcast.8), custom_call_target="tpu_custom_call" | custom-call | tf_op jit(solution)/shard_map/pallas_call | solution.py:212
  37.9 0.0 copy-start
  37.9 0.0 copy-start.1
  37.9 5.3 %all-to-all-start.1 = ((bf16[64,72,128]{2,1,0:T(8,128)(2,1)}), bf16[64,72,128]{2,1,0:T(8,128)(2,1)S(1)}, u32[]{:S(2)}, u32[]{:S(2)}) async-start(bf16[64,72,128]{2,1,0:T(8,128)(2,1)} %bitcast.5), calls=%async_computation.1 | async-start | bytes 2359296 | tf_op jit(solution)/shard_map/all_to_all | solution.py:223
  43.2 0.0 copy-done
  43.2 0.0 copy-done.1
  43.2 0.5 shard_map.55
  43.7 31.4 %all-to-all-done.1 = bf16[64,72,128]{2,1,0:T(8,128)(2,1)S(1)} async-done(((bf16[64,72,128]{2,1,0:T(8,128)(2,1)}), bf16[64,72,128]{2,1,0:T(8,128)(2,1)S(1)}, u32[]{:S(2)}, u32[]{:S(2)}) %all-to-all-start.1) | async-done | bytes 1179680 | tf_op jit(solution)/shard_map/all_to_all | solution.py:223
  75.1 1.9 %shard_map.58 = bf16[512,384]{1,0:T(8,128)(2,1)} custom-call(s32[1]{0:T(128)} %bitcast.start_ref, bf16[9,192,128]{2,1,0:T(8,128)(2,1)S(1)} %get-tuple-element.7.query_ref, bf16[9,192,128]{2,1,0:T(8,128)(2,1)S(1)} %get-tuple-element.8.grad_ref, bf16[64,9,8,128]{3,2,1,0:T(8,128)(2,1)S(1)} %bitcast.7), custom_call_target="tpu_custom_call" | custom-call | tf_op jit(solution)/shard_map/pallas_call | solution.py:237
Async XLA Ops:
  37.9 5.3 %copy-start = (bf16[512,384]{1,0:T(8,128)(2,1)S(1)}, bf16[512,384]{1,0:T(8,128)(2,1)}, u32[]{:S(2)}) copy-start(bf16[512,384]{1,0:T(8,128)(2,1)} %query_ref.1) | copy-start | bytes 1179652
  37.9 5.3 %copy-start.1 = (bf16[512,384]{1,0:T(8,128)(2,1)S(1)}, bf16[512,384]{1,0:T(8,128)(2,1)}, u32[]{:S(2)}) copy-start(bf16[512,384]{1,0:T(8,128)(2,1)} %grad_ref.1) | copy-start | bytes 1179652
  37.9 37.2 %all-to-all-start.1 = ((bf16[64,72,128]{2,1,0:T(8,128)(2,1)}), bf16[64,72,128]{2,1,0:T(8,128)(2,1)S(1)}, u32[]{:S(2)}, u32[]{:S(2)}) async-start(bf16[64,72,128]{2,1,0:T(8,128)(2,1)} %bitcast.5), calls=%async_computation.1 | async-start | bytes 2359296 | tf_op jit(solution)/shard_map/all_to_all | solution.py:223

commit v4 on v3

--- a/solution.py
+++ b/solution.py
@@ -19,8 +19,8 @@
 
 
 def pack_kernel(ids_hbm_ref, keys_ref, values_ref, out_ref, ids_ref, sems, ids_sem):
-    entries, pieces = keys_ref.shape[:2]
-    holders, chunks, piece, channels = out_ref.shape
+    entries, pieces, halves = keys_ref.shape[:3]
+    holders, chunks, rows, channels = out_ref.shape
     spans = ids_ref.shape[1]
     ids_copy = pltpu.make_async_copy(ids_hbm_ref, ids_ref, ids_sem)
     ids_copy.start()
@@ -29,20 +29,20 @@
         for n, ref in enumerate((keys_ref, values_ref)):
             copies.append(
                 pltpu.make_async_copy(
-                    ref.at[e], out_ref.at[pl.ds(n * pieces, pieces), e], sems.at[n, e]
+                    ref.at[e],
+                    out_ref.at[pl.ds(n * pieces, pieces), pl.ds(e * halves, halves)],
+                    sems.at[n, e],
                 )
             )
     for copy in copies:
         copy.start()
     ids_copy.wait()
-    lane = lax.broadcasted_iota(jnp.int32, (piece, channels), 1)
-    places = jnp.zeros((piece, channels), jnp.int32)
+    lane = lax.broadcasted_iota(jnp.int32, (rows, channels), 1)
+    places = jnp.zeros((rows, channels), jnp.int32)
     for c in range(2 * spans):
-        wanted_id = ids_ref[c % 2, c // 2]
-        place = (wanted_id // entries) * chunks + wanted_id % entries - holders * chunks // 2
-        places = jnp.where(lane == c, place, places)
+        places = jnp.where(lane == c, ids_ref[c % 2, c // 2] - holders * entries // 2, places)
     places = places.astype(jnp.float32).astype(jnp.bfloat16)
-    out_ref[:, entries] = jnp.broadcast_to(places[None], (holders, piece, channels))
+    out_ref[:, chunks - 1] = jnp.broadcast_to(places[None], (holders, rows, channels))
     for copy in copies:
         copy.wait()
 
@@ -178,8 +178,9 @@
     wanted = 2 * spans
     pieces = holders // 2
     piece = entry_rows // pieces
-    chunks = entries + 1
-    middle = holders * chunks // 2
+    rows = 2
+    halves = piece // rows
+    chunks = entries * halves + 1
     vmem = pl.BlockSpec(memory_space=pltpu.VMEM)
     smem = pl.BlockSpec(memory_space=pltpu.SMEM)
     hbm = pl.BlockSpec(memory_space=pltpu.HBM)
@@ -187,7 +188,7 @@
 
     packed = pl.pallas_call(
         pack_kernel,
-        out_shape=jax.ShapeDtypeStruct((holders, chunks, piece, channels), jnp.bfloat16),
+        out_shape=jax.ShapeDtypeStruct((holders, chunks, rows, channels), jnp.bfloat16),
         in_specs=[hbm] * 3,
         out_specs=vmem,
         scratch_shapes=[
@@ -200,26 +201,26 @@
         pltpu.with_memory_space_constraint(neighbour_ids.T, pltpu.HBM),
         *(
             pltpu.with_memory_space_constraint(
-                x.reshape(entries, pieces, piece, channels), pltpu.HBM
+                x.reshape(entries, pieces, halves, rows, channels), pltpu.HBM
             )
             for x in (cache_keys, cache_values)
         ),
     )
     spread = lax.all_to_all(packed, "db", split_axis=0, concat_axis=0, tiled=True)
-    places = (spread[:, entries, 0, :wanted].astype(jnp.int32) + middle) * 2
-    places = places.reshape(holders * wanted)
+    ids = spread[:, chunks - 1, 0, :wanted].astype(jnp.int32) + holders * entries // 2
+    places = (ids * halves + lax.div(ids, entries)).reshape(holders * wanted)
     places = jnp.concatenate([jnp.zeros((2,), jnp.int32), places])
     picked = pl.pallas_call(
         pick_kernel,
-        out_shape=jax.ShapeDtypeStruct((holders, 2 * (wanted + 2), piece // 2, channels), jnp.bfloat16),
+        out_shape=jax.ShapeDtypeStruct((holders, halves * (wanted + 2), rows, channels), jnp.bfloat16),
         in_specs=[smem, vmem],
         out_specs=hbm,
         scratch_shapes=[
-            pltpu.VMEM((holders, 2 * (wanted + 2), piece // 2, channels), jnp.bfloat16),
+            pltpu.VMEM((holders, halves * (wanted + 2), rows, channels), jnp.bfloat16),
             pltpu.SemaphoreType.DMA((4,)),
         ],
         compiler_params=small,
-    )(places, spread.reshape(holders * chunks * 2, piece // 2, channels))
+    )(places, spread.reshape(holders * chunks, rows, channels))
     arrived = lax.all_to_all(
         picked.reshape(holders, (wanted + 2) * piece, channels),
         "db", split_axis=0, concat_axis=0, tiled=True,

time: 77.8 us -> 77.3 us (level)
  no operation moved by 1% of the time
where the time goes in v4:
time: 77.3 us; the launch traced here: 76.3 us
  blocking collectives  33.9 us (44%)
  waiting for transfers between devices  31.4 us (41%)
  Pallas kernels  5.43 us (7%)
  starting transfers between devices  5.11 us (7%)
    all_to_all x1, blocking collectives, body(): lax.all_to_all(packed, 'db', split_axis=0, concat_axis=0, tiled=True)  33.9 us
    all_to_all x1, waiting for transfers between devices, body(): lax.all_to_all(picked.reshape(holders, (wanted + 2) * piece, channels), '...  31.4 us
    all_to_all x1, starting transfers between devices, body(): lax.all_to_all(picked.reshape(holders, (wanted + 2) * piece, channels), '...  5.11 us
    pallas_call x1, Pallas kernels, body(): pl.pallas_call(pick_kernel, out_shape=jax.ShapeDtypeStruct((holders, halv...  1.96 us
    pallas_call x1, Pallas kernels, body(): pl.pallas_call(attend_kernel, out_shape=jax.ShapeDtypeStruct((tokens, wid...  1.92 us
  transfers between devices with their start and end apart: 1, of which 1 were waited for; matrix products, arithmetic and copies ran while one was open for 0% of the time, Pallas kernels for 1%

profile of v4, /device:TPU:6, one launch (start us, length us, event | category | flops | bytes accessed | tf_op | source)
XLA Modules:
  0.0 76.3 jit_solution(18374560167750571319)
XLA Ops:
  0.0 1.0 %shard_map.56 = bf16[64,13,2,128]{3,2,1,0:T(2,128)(2,1)S(1)} custom-call(s32[2,8]{1,0:T(2,128)} %bitcast.11, bf16[6,32,2,2,128]{4,3,2,1,0:T(2,128)(2,1)} %bitcast.9, bf16[6,32,2,2,128]{4,3,2,1,0:T(2,128)(2,1)} %bitcast.10), custom_call_target="tpu_custom_call" | custom-call | tf_op jit(solution)/shard_map/pallas_call | solution.py:189
  1.1 33.9 %all_to_all.10 = bf16[64,13,2,128]{3,2,1,0:T(2,128)(2,1)S(1)} all-to-all(bf16[64,13,2,128]{3,2,1,0:T(2,128)(2,1)S(1)} %shard_map.56), channel_id=1, replica_groups=mesh['db'=64,'heads'=8] {'db'}, dimensions={0} | all-to-all | bytes 851968 | tf_op jit(solution)/shard_map/all_to_all | solution.py:209
  35.0 0.2 fusion.1
  35.2 0.1 add.20
  35.2 0.1 concatenate.3.index_ref
  35.3 2.0 %shard_map.57 = bf16[64,36,2,128]{3,2,1,0:T(2,128)(2,1)} custom-call(s32[1026]{0:T(1024)S(1)} %concatenate.3.index_ref, bf16[832,2,128]{2,1,0:T(2,128)(2,1)S(1)} %bitcast.8), custom_call_target="tpu_custom_call" | custom-call | tf_op jit(solution)/shard_map/pallas_call | solution.py:213
  37.3 0.0 copy-start
  37.3 0.0 copy-start.1
  37.3 5.1 %all-to-all-start.1 = ((bf16[64,72,128]{2,1,0:T(8,128)(2,1)}), bf16[64,72,128]{2,1,0:T(8,128)(2,1)S(1)}, u32[]{:S(2)}, u32[]{:S(2)}) async-start(bf16[64,72,128]{2,1,0:T(8,128)(2,1)} %bitcast.5), calls=%async_computation.1 | async-start | bytes 2359296 | tf_op jit(solution)/shard_map/all_to_all | solution.py:224
  42.4 0.0 copy-done
  42.4 0.0 copy-done.1
  42.5 0.5 shard_map.55
  43.0 31.4 %all-to-all-done.1 = bf16[64,72,128]{2,1,0:T(8,128)(2,1)S(1)} async-done(((bf16[64,72,128]{2,1,0:T(8,128)(2,1)}), bf16[64,72,128]{2,1,0:T(8,128)(2,1)S(1)}, u32[]{:S(2)}, u32[]{:S(2)}) %all-to-all-start.1) | async-done | bytes 1179680 | tf_op jit(solution)/shard_map/all_to_all | solution.py:224
  74.4 1.9 %shard_map.58 = bf16[512,384]{1,0:T(8,128)(2,1)} custom-call(s32[1]{0:T(128)} %bitcast.start_ref, bf16[9,192,128]{2,1,0:T(8,128)(2,1)S(1)} %get-tuple-element.7.query_ref, bf16[9,192,128]{2,1,0:T(8,128)(2,1)S(1)} %get-tuple-element.8.grad_ref, bf16[64,9,8,128]{3,2,1,0:T(8,128)(2,1)S(1)} %bitcast.7), custom_call_target="tpu_custom_call" | custom-call | tf_op jit(solution)/shard_map/pallas_call | solution.py:238
Async XLA Ops:
  37.3 5.2 %copy-start = (bf16[512,384]{1,0:T(8,128)(2,1)S(1)}, bf16[512,384]{1,0:T(8,128)(2,1)}, u32[]{:S(2)}) copy-start(bf16[512,384]{1,0:T(8,128)(2,1)} %query_ref.1) | copy-start | bytes 1179652
  37.3 5.2 %copy-start.1 = (bf16[512,384]{1,0:T(8,128)(2,1)S(1)}, bf16[512,384]{1,0:T(8,128)(2,1)}, u32[]{:S(2)}) copy-start(bf16[512,384]{1,0:T(8,128)(2,1)} %grad_ref.1) | copy-start | bytes 1179652
  37.3 37.1 %all-to-all-start.1 = ((bf16[64,72,128]{2,1,0:T(8,128)(2,1)}), bf16[64,72,128]{2,1,0:T(8,128)(2,1)S(1)}, u32[]{:S(2)}, u32[]{:S(2)}) async-start(bf16[64,72,128]{2,1,0:T(8,128)(2,1)} %bitcast.5), calls=%async_computation.1 | async-start | bytes 2359296 | tf_op jit(solution)/shard_map/all_to_all | solution.py:224

commit v5 on v4

v5 whole, which is shorter than its diff:
```python
import functools
import math

import jax
import jax.numpy as jnp
from jax import lax
from jax.experimental import pallas as pl
from jax.experimental.pallas import tpu as pltpu
from jax.sharding import PartitionSpec as P

HD = 128
GROUP = 3
SPAN = 64
LENGTH = 4096
TAIL = 8
AHEAD = 3
LAG = 2
SLOTS = AHEAD + LAG + 1
LAST_AT = 0


def exchange_order(holders):
    side = math.isqrt(holders)
    assert side * side == holders and side % 2 == 0
    along_z = [a // 2 + side // 2 * (a % 2) for a in range(side)]
    return [y * side + z for z in along_z for y in range(side)]


def place_of(holder, holders):
    side = math.isqrt(holders)
    y, z = lax.div(holder, side), lax.rem(holder, side)
    return (2 * lax.rem(z, side // 2) + lax.div(z, side // 2)) * side + y


def pack_kernel(_, ids_hbm_ref, keys_ref, values_ref, out_ref, ids_ref, sems, ids_sem):
    entries, pieces, halves = keys_ref.shape[:3]
    holders, chunks, rows, channels = out_ref.shape
    spans = ids_ref.shape[1]
    ids_copy = pltpu.make_async_copy(ids_hbm_ref, ids_ref, ids_sem)
    ids_copy.start()
    copies = []
    for e in range(entries):
        for n, ref in enumerate((keys_ref, values_ref)):
            copies.append(
                pltpu.make_async_copy(
                    ref.at[e],
                    out_ref.at[pl.ds(n * pieces, pieces), pl.ds(e * halves, halves)],
                    sems.at[n, e],
                )
            )
    for copy in copies:
        copy.start()
    ids_copy.wait()
    lane = lax.broadcasted_iota(jnp.int32, (rows, channels), 1)
    places = jnp.zeros((rows, channels), jnp.int32)
    for c in range(2 * spans):
        wanted_id = ids_ref[c % 2, c // 2]
        place = place_of(lax.div(wanted_id, entries), holders) * entries
        place = place + lax.rem(wanted_id, entries) - holders * entries // 2
        places = jnp.where(lane == c, place, places)
    places = places.astype(jnp.float32).astype(jnp.bfloat16)
    out_ref[:, chunks - 1] = jnp.broadcast_to(places[None], (holders, rows, channels))
    for copy in copies:
        copy.wait()


def pick_kernel(order, index_ref, table_ref, out_ref):
    dests, slots = out_ref.shape[0], out_ref.shape[1] // 2
    wanted = slots - 2
    for d in range(dests):
        before = order.index(order[d] - 1) if order[d] > 0 else d
        sources = [before * wanted + wanted - 2 + c for c in range(2)]
        sources += [d * wanted + c for c in range(wanted)]
        for c, source in enumerate(sources):
            out_ref[d, 2 * c : 2 * c + 2] = table_ref[pl.ds(index_ref[source], 2)]


def soften(scores, along):
    factor = 1.0 / math.sqrt(HD)
    highest = jnp.max(scores, axis=-1, keepdims=True)
    expo = jnp.exp2((scores - highest) * (factor / math.log(2.0)))
    scale = 1.0 / jnp.sum(expo, axis=-1, keepdims=True)
    delta = jnp.sum(expo * along, axis=-1, keepdims=True) * scale
    return (expo * (along - delta)).astype(jnp.bfloat16), scale * factor


def attend_kernel(start_ref, query_ref, grad_ref, rows_ref, out_ref, result_ref, scores_ref, along_ref, slope_ref, scale_ref, sems):
    tokens = out_ref.shape[0]
    blocks = tokens // SPAN
    pieces = rows_ref.shape[0] // 2
    half_shift = tokens // 2
    start = start_ref[0]
    row = lax.broadcasted_iota(jnp.int32, (SPAN, HD), 0)
    contract = (((1,), (1,)), ((), ()))

    def keys_of(n):
        return rows_ref[0:pieces, n].reshape(pieces * 8, HD)

    def parts(n):
        own = [(n * SPAN, (n + 1) * SPAN)] if n < blocks else []
        end = [(n * SPAN - TAIL, n * SPAN)] if n > 0 else []
        return own + end

    def height(n):
        return GROUP * sum(b - a for a, b in parts(n))

    def products(n, slot):
        values = rows_ref[pieces : 2 * pieces, n].reshape(pieces * 8, HD)
        for ref, other, out in ((query_ref, keys_of(n), scores_ref), (grad_ref, values, along_ref)):
            rows = [
                ref[a:b, g * HD : (g + 1) * HD] for a, b in parts(n) for g in range(GROUP)
            ]
            out[slot, : height(n)] = lax.dot_general(
                jnp.concatenate(rows, axis=0), other, contract, preferred_element_type=jnp.float32
            )

    def softened(n, slot):
        total = height(n)
        slope, scale = soften(scores_ref[slot, :total], along_ref[slot, :total])
        slope_ref[slot, :total] = slope
        scale_ref[slot, :total] = jnp.broadcast_to(scale, (total, HD))

    def finished(n, slot):
        total = height(n)
        result = (
            jnp.dot(slope_ref[slot, :total], keys_of(n), preferred_element_type=jnp.float32)
            * scale_ref[slot, :total]
        )
        split, at = [], 0
        for a, b in parts(n):
            split.append([result[at + g * (b - a) : at + (g + 1) * (b - a)] for g in range(GROUP)])
            at += GROUP * (b - a)
        return split

    order = [n for n in range(blocks)]
    order.insert(LAST_AT, blocks)
    done_of, copies = {}, []
    for at in range(-AHEAD, len(order) + LAG):
        if 0 <= at + AHEAD < len(order):
            products(order[at + AHEAD], (at + AHEAD) % SLOTS)
        if 0 <= at < len(order):
            softened(order[at], at % SLOTS)
        if at < LAG:
            continue
        done = order[at - LAG]
        done_of[done] = finished(done, (at - LAG) % SLOTS)
        for n in range(1, blocks + 1):
            if done not in (n, n - 1) or n not in done_of or n - 1 not in done_of:
                continue
            token = start + (n - 1) * SPAN
            idle = (token == 0) | ((token + half_shift) % LENGTH == 0)
            kept = row >= jnp.where(idle, SPAN - 1, 0)
            for g in range(GROUP):
                before, after = done_of[n - 1][0][g], done_of[n][-1][g]
                end = jnp.where(row[-8:] == SPAN - 1, after[-8:], before[-8:])
                here = jnp.concatenate([before[:-8], end], axis=0)
                result_ref[(n - 1) * SPAN : n * SPAN, g * HD : (g + 1) * HD] = jnp.where(
                    kept, here, 0.0
                ).astype(out_ref.dtype)
            rows = pl.ds((n - 1) * SPAN, SPAN)
            copies.append(
                pltpu.make_async_copy(result_ref.at[rows], out_ref.at[rows], sems.at[n - 1])
            )
            copies[-1].start()
    for copy in copies:
        copy.wait()


def body(queries, neighbour_ids, cache_keys, cache_values, out_grad):
    holders = lax.axis_size("db")
    me = lax.axis_index("db")
    entries, entry_rows, channels = cache_keys.shape
    tokens, width = queries.shape
    spans = neighbour_ids.shape[0]
    wanted = 2 * spans
    pieces = holders // 2
    piece = entry_rows // pieces
    rows = 2
    halves = piece // rows
    chunks = entries * halves + 1
    order = exchange_order(holders)
    vmem = pl.BlockSpec(memory_space=pltpu.VMEM)
    smem = pl.BlockSpec(memory_space=pltpu.SMEM)
    hbm = pl.BlockSpec(memory_space=pltpu.HBM)
    small = pltpu.CompilerParams(vmem_limit_bytes=16 * 2**20)

    start = (me * tokens).reshape(1).astype(jnp.int32)
    packed = pl.pallas_call(
        pack_kernel,
        out_shape=jax.ShapeDtypeStruct((holders, chunks, rows, channels), jnp.bfloat16),
        in_specs=[smem] + [hbm] * 3,
        out_specs=vmem,
        scratch_shapes=[
            pltpu.SMEM((2, spans), jnp.int32),
            pltpu.SemaphoreType.DMA((2, entries)),
            pltpu.SemaphoreType.DMA,
        ],
        compiler_params=small,
    )(
        start,
        pltpu.with_memory_space_constraint(neighbour_ids.T, pltpu.HBM),
        *(
            pltpu.with_memory_space_constraint(
                x.reshape(entries, pieces, halves, rows, channels), pltpu.HBM
            )
            for x in (cache_keys, cache_values)
        ),
    )
    exchange = functools.partial(
        lax.all_to_all, axis_name="db", split_axis=0, concat_axis=0, tiled=True, axis_index_groups=[order]
    )
    spread = exchange(packed)
    ids = spread[:, chunks - 1, 0, :wanted].astype(jnp.int32) + holders * entries // 2
    places = (ids * halves + lax.div(ids, entries)).reshape(holders * wanted)
    picked = pl.pallas_call(
        functools.partial(pick_kernel, order),
        out_shape=jax.ShapeDtypeStruct((holders, halves * (wanted + 2), rows, channels), jnp.bfloat16),
        in_specs=[smem, vmem],
        out_specs=vmem,
        compiler_params=small,
    )(places, spread.reshape(holders * chunks, rows, channels))
    arrived = exchange(picked.reshape(holders, (wanted + 2) * piece, channels)).reshape(
        holders, spans + 1, 2 * piece, channels
    )
    return pl.pallas_call(
        attend_kernel,
        out_shape=jax.ShapeDtypeStruct((tokens, width), jnp.bfloat16),
        in_specs=[smem] + [vmem] * 3,
        out_specs=hbm,
        scratch_shapes=[
            pltpu.VMEM((tokens, width), jnp.bfloat16),
            pltpu.VMEM((SLOTS, GROUP * (SPAN + TAIL), 2 * entry_rows), jnp.float32),
            pltpu.VMEM((SLOTS, GROUP * (SPAN + TAIL), 2 * entry_rows), jnp.float32),
            pltpu.VMEM((SLOTS, GROUP * (SPAN + TAIL), 2 * entry_rows), jnp.bfloat16),
            pltpu.VMEM((SLOTS, GROUP * (SPAN + TAIL), HD), jnp.float32),
            pltpu.SemaphoreType.DMA((spans,)),
        ],
        compiler_params=small,
    )(start, queries, out_grad, arrived)


def solution(mesh):
    return jax.shard_map(
        body,
        mesh=mesh,
        in_specs=(
            P("db", "heads"),
            P("db", None),
            P("db", None, "heads"),
            P("db", None, "heads"),
            P("db", "heads"),
        ),
        out_specs=P("db", "heads"),
        check_vma=False,
    )
```

time: 77.3 us -> 75.3 us (0.974)
  blocking collectives: 33.9 us -> 69.4 us
  waiting for transfers between devices: 31.4 us -> 0 us
  starting transfers between devices: 5.11 us -> 0 us
  Pallas kernels: 5.43 us -> 4.43 us
    all_to_all x1 -> x2, blocking collectives: 33.9 us -> 69.4 us  [the longest x1 35.9 us: body(): exchange(picked.reshape(holders, (wanted + 2) * piece, channels))]
    all_to_all x1 -> x0, waiting for transfers between devices: 31.4 us -> none  [body(): lax.all_to_all(picked.reshape(holders, (wanted + 2) * piece, channels), '...]
    all_to_all x1 -> x0, starting transfers between devices: 5.11 us -> none  [body(): lax.all_to_all(picked.reshape(holders, (wanted + 2) * piece, channels), '...]
    pallas_call x2 -> x1, Pallas kernels: 2.46 us -> 1.21 us  [body(): pl.pallas_call(functools.partial(pick_kernel, order), out_shape=jax.Shape...]
  transfers between devices with their start and end apart: 1 -> 0, of which waited for: 1 -> 0; matrix products, arithmetic and copies ran while one was open for 0% -> 0% of each run, Pallas kernels for 1% -> 0%
where the time goes in v5:
time: 75.3 us; the launch traced here: 74.1 us
  blocking collectives  69.4 us (92%)
  Pallas kernels  4.43 us (6%)
    all_to_all x1, blocking collectives, body(): exchange(picked.reshape(holders, (wanted + 2) * piece, channels))  35.9 us
    all_to_all x1, blocking collectives, body(): spread = exchange(packed)  33.5 us
    pallas_call x1, Pallas kernels, body(): pl.pallas_call(attend_kernel, out_shape=jax.ShapeDtypeStruct((tokens, wid...  2.09 us

profile of v5, /device:TPU:6, one launch (start us, length us, event | category | flops | bytes accessed | tf_op | source)
XLA Modules:
  0.0 74.1 jit_solution(1076726207570610625)
XLA Ops:
  0.0 1.1 %shard_map.55 = bf16[64,13,2,128]{3,2,1,0:T(2,128)(2,1)S(1)} custom-call(s32[1]{0:T(128)} %bitcast._.start_ref, s32[2,8]{1,0:T(2,128)} %bitcast.12, bf16[6,32,2,2,128]{4,3,2,1,0:T(2,128)(2,1)} %bitcast.10, bf16[6,32,2,2,128]{4,3,2,1,0:T(2,128)(2,1)} %bitcast.11), custom_call_target="tpu_custom_call" | custom-call | tf_op jit(solution)/shard_map/pallas_call | solution.py:188
  1.1 33.5 %all_to_all.10 = bf16[64,13,2,128]{3,2,1,0:T(2,128)(2,1)S(1)} all-to-all(bf16[64,13,2,128]{3,2,1,0:T(2,128)(2,1)S(1)} %shard_map.55), channel_id=1, replica_groups={{0,64,128,192,256,320,384,448,32,96,160,224,288,352,416,480,8,72,136,20..., dimensions={0} | all-to-all | bytes 851968 | tf_op jit(solution)/shard_map/all_to_all | solution.py:212
  34.6 0.2 fusion.1
  34.8 0.1 add.18.index_ref
  34.9 1.2 %shard_map.56 = bf16[64,36,2,128]{3,2,1,0:T(2,128)(2,1)S(1)} custom-call(s32[1024]{0:T(1024)S(1)} %add.18.index_ref, bf16[832,2,128]{2,1,0:T(2,128)(2,1)S(1)} %bitcast.9), custom_call_target="tpu_custom_call" | custom-call | tf_op jit(solution)/shard_map/pallas_call | solution.py:215
  36.1 0.0 copy-start
  36.1 0.0 copy-start.1
  36.1 35.9 %all_to_all.11 = bf16[64,72,128]{2,1,0:T(8,128)(2,1)S(1)} all-to-all(bf16[64,72,128]{2,1,0:T(8,128)(2,1)S(1)} %bitcast.8), channel_id=1, replica_groups={{0,64,128,192,256,320,384,448,32,96,160,224,288,352,416,480,8,72,136,20..., dimensions={0} | all-to-all | bytes 2359296 | tf_op jit(solution)/shard_map/all_to_all | solution.py:222
  72.0 0.0 copy-done
  72.0 0.0 copy-done.1
  72.1 2.1 %shard_map.57 = bf16[512,384]{1,0:T(8,128)(2,1)} custom-call(s32[1]{0:T(128)} %bitcast._.start_ref, bf16[512,384]{1,0:T(8,128)(2,1)S(1)} %copy-done, bf16[512,384]{1,0:T(8,128)(2,1)S(1)} %copy-done.1, bf16[64,9,8,128]{3,2,1,0:T(8,128)(2,1)S(1)} %bitcast.7), custom_call_target="tpu_custom_call" | custom-call | tf_op jit(solution)/shard_map/pallas_call | solution.py:225
Async XLA Ops:
  36.1 36.0 %copy-start = (bf16[512,384]{1,0:T(8,128)(2,1)S(1)}, bf16[512,384]{1,0:T(8,128)(2,1)}, u32[]{:S(2)}) copy-start(bf16[512,384]{1,0:T(8,128)(2,1)} %query_ref.1) | copy-start | bytes 1179652
  36.1 35.9 %copy-start.1 = (bf16[512,384]{1,0:T(8,128)(2,1)S(1)}, bf16[512,384]{1,0:T(8,128)(2,1)}, u32[]{:S(2)}) copy-start(bf16[512,384]{1,0:T(8,128)(2,1)} %grad_ref.1) | copy-start | bytes 1179652

commit v6 on v5

--- a/solution.py
+++ b/solution.py
@@ -21,15 +21,17 @@
 
 def exchange_order(holders):
     side = math.isqrt(holders)
-    assert side * side == holders and side % 2 == 0
-    along_z = [a // 2 + side // 2 * (a % 2) for a in range(side)]
-    return [y * side + z for z in along_z for y in range(side)]
+    half = side // 2
+    assert side * side == holders and side == 2 * half
+    along_z = [a // 2 + half * ((a + 1) % 2) for a in range(side)]
+    return [(b + half) % side * side + z for z in along_z for b in range(side)]
 
 
 def place_of(holder, holders):
     side = math.isqrt(holders)
+    half = side // 2
     y, z = lax.div(holder, side), lax.rem(holder, side)
-    return (2 * lax.rem(z, side // 2) + lax.div(z, side // 2)) * side + y
+    return (2 * lax.rem(z, half) + 1 - lax.div(z, half)) * side + lax.rem(y + half, side)
 
 
 def pack_kernel(_, ids_hbm_ref, keys_ref, values_ref, out_ref, ids_ref, sems, ids_sem):

time: 75.3 us -> 73 us (0.969); the launches traced: 74.1 us -> 72.8 us
  blocking collectives: 69.4 us -> 68 us
    all_to_all x1, blocking collectives: 33.5 us -> 29.4 us  [body(): spread = exchange(packed)]
    all_to_all x1, blocking collectives: 35.9 us -> 38.6 us  [body(): exchange(picked.reshape(holders, (wanted + 2) * piece, channels))]
where the time goes in v6:
time: 73 us; the launch traced here: 72.8 us
  blocking collectives  68 us (93%)
  Pallas kernels  4.47 us (6%)
    all_to_all x1, blocking collectives, body(): exchange(picked.reshape(holders, (wanted + 2) * piece, channels))  38.6 us
    all_to_all x1, blocking collectives, body(): spread = exchange(packed)  29.4 us
    pallas_call x1, Pallas kernels, body(): pl.pallas_call(attend_kernel, out_shape=jax.ShapeDtypeStruct((tokens, wid...  2.09 us

profile of v6, /device:TPU:6, one launch (start us, length us, event | category | flops | bytes accessed | tf_op | source)
XLA Modules:
  0.0 72.8 jit_solution(13601143476832457329)
XLA Ops:
  0.0 1.2 %shard_map.55 = bf16[64,13,2,128]{3,2,1,0:T(2,128)(2,1)S(1)} custom-call(s32[1]{0:T(128)} %bitcast._.start_ref, s32[2,8]{1,0:T(2,128)} %bitcast.12, bf16[6,32,2,2,128]{4,3,2,1,0:T(2,128)(2,1)} %bitcast.10, bf16[6,32,2,2,128]{4,3,2,1,0:T(2,128)(2,1)} %bitcast.11), custom_call_target="tpu_custom_call" | custom-call | tf_op jit(solution)/shard_map/pallas_call | solution.py:190
  1.2 29.4 %all_to_all.10 = bf16[64,13,2,128]{3,2,1,0:T(2,128)(2,1)S(1)} all-to-all(bf16[64,13,2,128]{3,2,1,0:T(2,128)(2,1)S(1)} %shard_map.55), channel_id=1, replica_groups={{288,352,416,480,32,96,160,224,256,320,384,448,0,64,128,192,296,360,424..., dimensions={0} | all-to-all | bytes 851968 | tf_op jit(solution)/shard_map/all_to_all | solution.py:214
  30.6 0.2 fusion.1
  30.8 0.1 add.18.index_ref
  30.9 1.2 %shard_map.56 = bf16[64,36,2,128]{3,2,1,0:T(2,128)(2,1)S(1)} custom-call(s32[1024]{0:T(1024)S(1)} %add.18.index_ref, bf16[832,2,128]{2,1,0:T(2,128)(2,1)S(1)} %bitcast.9), custom_call_target="tpu_custom_call" | custom-call | tf_op jit(solution)/shard_map/pallas_call | solution.py:217
  32.1 0.0 copy-start
  32.1 0.0 copy-start.1
  32.1 38.6 %all_to_all.11 = bf16[64,72,128]{2,1,0:T(8,128)(2,1)S(1)} all-to-all(bf16[64,72,128]{2,1,0:T(8,128)(2,1)S(1)} %bitcast.8), channel_id=1, replica_groups={{288,352,416,480,32,96,160,224,256,320,384,448,0,64,128,192,296,360,424..., dimensions={0} | all-to-all | bytes 2359296 | tf_op jit(solution)/shard_map/all_to_all | solution.py:224
  70.7 0.0 copy-done
  70.7 0.0 copy-done.1
  70.7 2.1 %shard_map.57 = bf16[512,384]{1,0:T(8,128)(2,1)} custom-call(s32[1]{0:T(128)} %bitcast._.start_ref, bf16[512,384]{1,0:T(8,128)(2,1)S(1)} %copy-done, bf16[512,384]{1,0:T(8,128)(2,1)S(1)} %copy-done.1, bf16[64,9,8,128]{3,2,1,0:T(8,128)(2,1)S(1)} %bitcast.7), custom_call_target="tpu_custom_call" | custom-call | tf_op jit(solution)/shard_map/pallas_call | solution.py:227
Async XLA Ops:
  32.1 38.6 %copy-start = (bf16[512,384]{1,0:T(8,128)(2,1)S(1)}, bf16[512,384]{1,0:T(8,128)(2,1)}, u32[]{:S(2)}) copy-start(bf16[512,384]{1,0:T(8,128)(2,1)} %query_ref.1) | copy-start | bytes 1179652
  32.1 38.6 %copy-start.1 = (bf16[512,384]{1,0:T(8,128)(2,1)S(1)}, bf16[512,384]{1,0:T(8,128)(2,1)}, u32[]{:S(2)}) copy-start(bf16[512,384]{1,0:T(8,128)(2,1)} %grad_ref.1) | copy-start | bytes 1179652

commit v7 on v6

--- a/solution.py
+++ b/solution.py
@@ -23,15 +23,15 @@
     side = math.isqrt(holders)
     half = side // 2
     assert side * side == holders and side == 2 * half
-    along_z = [a // 2 + half * ((a + 1) % 2) for a in range(side)]
+    along_z = [(a // 2 + half * (a % 2) + side - 2) % side for a in range(side)]
     return [(b + half) % side * side + z for z in along_z for b in range(side)]
 
 
 def place_of(holder, holders):
     side = math.isqrt(holders)
     half = side // 2
-    y, z = lax.div(holder, side), lax.rem(holder, side)
-    return (2 * lax.rem(z, half) + 1 - lax.div(z, half)) * side + lax.rem(y + half, side)
+    y, z = lax.div(holder, side), lax.rem(holder + 2, side)
+    return (2 * lax.rem(z, half) + lax.div(z, half)) * side + lax.rem(y + half, side)
 
 
 def pack_kernel(_, ids_hbm_ref, keys_ref, values_ref, out_ref, ids_ref, sems, ids_sem):

time: 73 us -> 73.2 us (level)
  no operation moved by 1% of the time
where the time goes in v7:
time: 73.2 us; the launch traced here: 72.9 us
  blocking collectives  68.1 us (93%)
  Pallas kernels  4.48 us (6%)
    all_to_all x1, blocking collectives, body(): exchange(picked.reshape(holders, (wanted + 2) * piece, channels))  38.3 us
    all_to_all x1, blocking collectives, body(): spread = exchange(packed)  29.8 us
    pallas_call x1, Pallas kernels, body(): pl.pallas_call(attend_kernel, out_shape=jax.ShapeDtypeStruct((tokens, wid...  2.09 us

profile of v7, /device:TPU:6, one launch (start us, length us, event | category | flops | bytes accessed | tf_op | source)
XLA Modules:
  0.0 72.9 jit_solution(3802598483828413977)
XLA Ops:
  0.0 1.2 %shard_map.55 = bf16[64,13,2,128]{3,2,1,0:T(2,128)(2,1)S(1)} custom-call(s32[1]{0:T(128)} %bitcast._.start_ref, s32[2,8]{1,0:T(2,128)} %bitcast.12, bf16[6,32,2,2,128]{4,3,2,1,0:T(2,128)(2,1)} %bitcast.10, bf16[6,32,2,2,128]{4,3,2,1,0:T(2,128)(2,1)} %bitcast.11), custom_call_target="tpu_custom_call" | custom-call | tf_op jit(solution)/shard_map/pallas_call | solution.py:190
  1.2 29.8 %all_to_all.10 = bf16[64,13,2,128]{3,2,1,0:T(2,128)(2,1)S(1)} all-to-all(bf16[64,13,2,128]{3,2,1,0:T(2,128)(2,1)S(1)} %shard_map.55), channel_id=1, replica_groups={{304,368,432,496,48,112,176,240,272,336,400,464,16,80,144,208,312,376,4..., dimensions={0} | all-to-all | bytes 851968 | tf_op jit(solution)/shard_map/all_to_all | solution.py:214
  31.0 0.2 fusion.1
  31.2 0.1 add.18.index_ref
  31.3 1.2 %shard_map.56 = bf16[64,36,2,128]{3,2,1,0:T(2,128)(2,1)S(1)} custom-call(s32[1024]{0:T(1024)S(1)} %add.18.index_ref, bf16[832,2,128]{2,1,0:T(2,128)(2,1)S(1)} %bitcast.9), custom_call_target="tpu_custom_call" | custom-call | tf_op jit(solution)/shard_map/pallas_call | solution.py:217
  32.5 0.0 copy-start
  32.5 0.0 copy-start.1
  32.5 38.3 %all_to_all.11 = bf16[64,72,128]{2,1,0:T(8,128)(2,1)S(1)} all-to-all(bf16[64,72,128]{2,1,0:T(8,128)(2,1)S(1)} %bitcast.8), channel_id=1, replica_groups={{304,368,432,496,48,112,176,240,272,336,400,464,16,80,144,208,312,376,4..., dimensions={0} | all-to-all | bytes 2359296 | tf_op jit(solution)/shard_map/all_to_all | solution.py:224
  70.9 0.0 copy-done
  70.9 0.0 copy-done.1
  70.9 2.1 %shard_map.57 = bf16[512,384]{1,0:T(8,128)(2,1)} custom-call(s32[1]{0:T(128)} %bitcast._.start_ref, bf16[512,384]{1,0:T(8,128)(2,1)S(1)} %copy-done, bf16[512,384]{1,0:T(8,128)(2,1)S(1)} %copy-done.1, bf16[64,9,8,128]{3,2,1,0:T(8,128)(2,1)S(1)} %bitcast.7), custom_call_target="tpu_custom_call" | custom-call | tf_op jit(solution)/shard_map/pallas_call | solution.py:227
Async XLA Ops:
  32.5 38.3 %copy-start = (bf16[512,384]{1,0:T(8,128)(2,1)S(1)}, bf16[512,384]{1,0:T(8,128)(2,1)}, u32[]{:S(2)}) copy-start(bf16[512,384]{1,0:T(8,128)(2,1)} %query_ref.1) | copy-start | bytes 1179652
  32.5 38.3 %copy-start.1 = (bf16[512,384]{1,0:T(8,128)(2,1)S(1)}, bf16[512,384]{1,0:T(8,128)(2,1)}, u32[]{:S(2)}) copy-start(bf16[512,384]{1,0:T(8,128)(2,1)} %grad_ref.1) | copy-start | bytes 1179652
